TPU v7x, 128 devices: a whole 4x4x4 slice. The times are simulated.
128 devices in a mesh: member: 8 (over y, core), tile: 16 (over z, x).
Axes of the slice: x: 4, y: 4, z: 4, core: 2. Of those that a mesh axis runs over, the one named last changes fastest.
Arguments:
- perturb: bfloat16 [128, 256, 2560], P('member', 'tile'), may hold values from -0.5 to 0.5
- weights: float32 [128, 64, 1280], P('member', 'tile'), may hold values from -1.2 to 1.2
- column_map: bfloat16 [1280, 2560], replicated, may hold values from -0.15625 to 0.15625
- background: float32 [256, 2560], P('tile', 'member'), may hold values from -6 to 6
- stencil_index: int32 [16, 128, 8, 8], P('tile'), may hold values from 0 to 4798, as said below
- row_fraction: float32 [16, 128, 8, 8], P('tile'), may hold values from 0 to 1
- column_fraction: float32 [16, 128, 8, 8], P('tile'), may hold values from 0 to 1
- block_lengths: int32 [16, 128, 8], P('tile'), may hold values from 0 to 8, as said below
- obs_value: float32 [128, 128, 8], P(('member', 'tile')), may hold values from -6 to 6
- obs_error: float32 [128, 128, 8], P(('member', 'tile')), may hold values from 0.3 to 1
- instrument_gain: float32 [128], P(('member', 'tile')), may hold values from 0.2 to 0.8
Outputs:
- analysis_weights: float32 [128, 64, 1280], P('member', 'tile')
- analysis_increment: float32 [256, 2560], P('tile', 'member')
Inputs may be any that keep to these rules, and one draw needn't show every extreme that they name: stencil_index = r * 320 + c with 0 <= r < 15 and 0 <= c < 319. `block_lengths`: in every draw some owner (one tile and one member index) has all its blocks full.
All inputs are finite; a program needn't handle non-finite values.
Results may differ from a plain program's by a relative error of at most 0.0022.
Values may be sent and summed in bfloat16 or wider, within the bound.
No kernel may reach another device: no remote copies, remote signals or barrier semaphores. Data moves between devices by JAX's collectives and lax.ppermute only.
A program may use at most 64 MiB of HBM per device.

v0:
```python
import jax
import jax.numpy as jnp
from jax import lax
from jax.sharding import PartitionSpec as P

RATIO = 4
KSM = 3
DIFFUSION = 0.45


def padded_2(block, sides, width):
    for axis, dim in sides:
        count = lax.axis_size(axis)
        forward = [(i, i + 1) for i in range(count - 1)]
        backward = [(target, source) for source, target in forward]
        low = lax.ppermute(
            lax.slice_in_dim(block, block.shape[dim] - width, None, axis=dim), axis, forward
        )
        high = lax.ppermute(lax.slice_in_dim(block, 0, width, axis=dim), axis, backward)
        block = jnp.concatenate([low, block, high], axis=dim)
    return block


def rows_halo(grid_values, width_rows):
    return padded_2(grid_values, (("tile", 1),), width_rows)


def smoothed(grid_values, extra_rows):
    for pass_index in range(KSM):
        padded = rows_halo(grid_values, 1)
        grid_values = grid_values + DIFFUSION * (padded[:, :-2] + padded[:, 2:] - 2.0 * grid_values)
    if extra_rows > 0:
        rounded_rows = grid_values.astype(jnp.bfloat16)
        grid_values = padded_2(rounded_rows, (("tile", 1),), extra_rows)
    return grid_values


def refine(extended):
    members_here, row_count, col_count = extended.shape
    lower_rows = extended[:, :-2]
    middle = extended[:, 1:-1]
    upper_rows = extended[:, 2:]
    pieces = []
    for offset in range(RATIO):
        shift_value = (offset + 0.5) / RATIO - 0.5
        if shift_value < 0:
            pieces.append((1.0 + shift_value) * middle - shift_value * lower_rows)
        else:
            pieces.append((1.0 - shift_value) * middle + shift_value * upper_rows)
    return jnp.stack(pieces, axis=2).reshape(members_here, (row_count - 2) * RATIO, col_count)


def refine_adjoint(fine_field):
    members_here, fine_count, col_count = fine_field.shape
    row_count = fine_count // RATIO
    blocks = fine_field.reshape(members_here, row_count, RATIO, col_count)
    middle = jnp.zeros_like(blocks[:, :, 0])
    lower_rows = jnp.zeros_like(middle)
    upper_rows = jnp.zeros_like(middle)
    for offset in range(RATIO):
        shift_value = (offset + 0.5) / RATIO - 0.5
        fine_layer = blocks[:, :, offset]
        if shift_value < 0:
            middle = middle + (1.0 + shift_value) * fine_layer
            lower_rows = lower_rows - shift_value * fine_layer
        else:
            middle = middle + (1.0 - shift_value) * fine_layer
            upper_rows = upper_rows + shift_value * fine_layer
    return (
        jnp.pad(middle, ((0, 0), (1, 1), (0, 0)))
        + jnp.pad(lower_rows, ((0, 0), (0, 2), (0, 0)))
        + jnp.pad(upper_rows, ((0, 0), (2, 0), (0, 0)))
    )


def forward(coarse, perturb, column_map):
    extended = smoothed(coarse, 1)
    members_here, row_count, coarse_cols = extended.shape
    mapped = jnp.dot(
        extended.reshape(-1, coarse_cols), column_map, preferred_element_type=jnp.float32
    )
    fine_field = refine(mapped.reshape(members_here, row_count, -1))
    member_term = jnp.sum(fine_field * perturb, axis=0)
    return lax.psum_scatter(member_term, "member", scatter_dimension=1, tiled=True)


def adjoint_map(spread_field, perturb, column_map):
    edge_terms = refine_adjoint(perturb * spread_field)
    rim_rows = jnp.stack([edge_terms[:, 0], edge_terms[:, -1]], axis=1)
    beside_all = rows_halo(rim_rows, 1)
    inner_rows = edge_terms[:, 1:-1]
    inner_rows = inner_rows.at[:, 0].add(beside_all[:, 0]).at[:, -1].add(beside_all[:, 3])
    members_here, row_count, fine_cols = inner_rows.shape
    pulled = lax.dot_general(
        inner_rows.astype(jnp.bfloat16).reshape(-1, fine_cols),
        column_map,
        (((1,), (1,)), ((), ())),
        preferred_element_type=jnp.float32,
    )
    return smoothed(pulled.reshape(members_here, row_count, -1), 0)


def bilinear_factors(index, row_frac, column_frac, region_width, row_count):
    row_pos = (index // region_width)[..., None]
    column_pos = (index % region_width)[..., None]
    row_ids = lax.broadcasted_iota(jnp.int32, index.shape + (row_count,), index.ndim)
    column_ids = lax.broadcasted_iota(jnp.int32, index.shape + (region_width,), index.ndim)
    row_factor = jnp.where(row_ids == row_pos, 1.0 - row_frac[..., None], 0.0) + jnp.where(
        row_ids == row_pos + 1, row_frac[..., None], 0.0
    )
    column_factor = jnp.where(
        column_ids == column_pos, 1.0 - column_frac[..., None], 0.0
    ) + jnp.where(column_ids == column_pos + 1, column_frac[..., None], 0.0)
    return (row_factor, column_factor)


def interpolate_region(field_region, index, row_frac, column_frac):
    row_count, region_width = field_region.shape
    row_factor, column_factor = bilinear_factors(
        index, row_frac, column_frac, region_width, row_count
    )
    along = jnp.einsum("bsr,rc->bsc", row_factor, field_region, precision=lax.Precision.HIGHEST)
    return jnp.sum(along * column_factor, axis=-1)


def spread_tile(residual, index, row_frac, column_frac, region_width, row_count):
    row_factor, column_factor = bilinear_factors(
        index, row_frac, column_frac, region_width, row_count
    )
    weighted = row_factor * residual[..., None]
    regions = jnp.einsum("bmsr,bmsc->rmc", weighted, column_factor, precision=lax.Precision.HIGHEST)
    return regions.reshape(row_count, -1)


def innovation(obs_state, obs_value, obs_error, instrument):
    bounded = jnp.tanh(obs_state)
    derivative = 1.0 + instrument * (1.0 - bounded * bounded)
    misfit = obs_state + instrument * bounded - obs_value
    precision_obs = 1.0 / (obs_error * obs_error)
    return (derivative * misfit * precision_obs, derivative * derivative * precision_obs)


def global_sum(values):
    return lax.psum(values, ("member", "tile"))


def shards(
    perturb,
    weights,
    column_map,
    background,
    stencil_index,
    row_fraction,
    column_fraction,
    block_lengths,
    obs_value,
    obs_error,
    instrument_gain,
):
    member_pos = lax.axis_index("member")
    member_count = lax.axis_size("member")
    tile_count = lax.axis_size("tile")
    fine_rows, region_width = background.shape
    local_index = stencil_index[0]
    local_row = row_fraction[0]
    local_col = column_fraction[0]
    slot_ids = lax.broadcasted_iota(jnp.int32, local_index.shape, 2)
    valid_slots = (slot_ids < block_lengths[0][:, :, None]).astype(jnp.float32)
    own_index = lax.dynamic_index_in_dim(local_index, member_pos, 1, False)
    own_row = lax.dynamic_index_in_dim(local_row, member_pos, 1, False)
    own_col = lax.dynamic_index_in_dim(local_col, member_pos, 1, False)
    own_valid = lax.dynamic_index_in_dim(valid_slots, member_pos, 1, False)

    def fan_out(values):
        arranged = jnp.transpose(values.reshape(member_count, tile_count, -1), (1, 0, 2))
        widened = jnp.broadcast_to(arranged[None], (member_count,) + arranged.shape)
        return widened.reshape(member_count * tile_count, member_count, -1)

    coarse = weights
    increment = forward(coarse, perturb, column_map)
    obs_state = interpolate_region(background + increment, own_index, own_row, own_col)
    received = lax.all_to_all(
        obs_state, ("member", "tile"), split_axis=0, concat_axis=0, tiled=True
    )
    residual, obs_weight = innovation(received, obs_value[0], obs_error[0], instrument_gain[0])
    residual, obs_weight = (
        lax.all_to_all(
            fan_out(residual), ("member", "tile"), split_axis=0, concat_axis=0, tiled=True
        ),
        lax.all_to_all(
            fan_out(obs_weight), ("member", "tile"), split_axis=0, concat_axis=0, tiled=True
        ),
    )
    spread_field = spread_tile(
        residual * valid_slots, local_index, local_row, local_col, region_width, fine_rows
    )
    gradient = coarse + adjoint_map(spread_field, perturb, column_map)
    grad_square = jnp.sum(gradient * gradient)
    grad_total = global_sum(grad_square)
    grad_image = forward(gradient, perturb, column_map)
    grad_obs = interpolate_region(grad_image, own_index, own_row, own_col)
    own_weight = lax.dynamic_index_in_dim(obs_weight, member_pos, 1, False)
    curvature = jnp.sum(own_valid * own_weight * grad_obs * grad_obs)
    curve_total = global_sum(curvature)
    step_size = grad_total / (grad_total + curve_total)
    coarse = coarse - step_size * gradient
    increment = increment - step_size * grad_image
    return (coarse, increment)


def solution(mesh):
    placed = (
        P("member", "tile", None),
        P("member", "tile", None),
        P(),
        P("tile", "member"),
        P("tile", None, None, None),
        P("tile", None, None, None),
        P("tile", None, None, None),
        P("tile", None, None),
        P(("member", "tile"), None, None),
        P(("member", "tile"), None, None),
        P(("member", "tile")),
    )
    return jax.shard_map(
        shards,
        mesh=mesh,
        in_specs=placed,
        out_specs=(P("member", "tile", None), P("tile", "member")),
        check_vma=False,
    )
```

profile of v0, /device:TPU:1, one launch (start us, length us, event | category | flops | bytes accessed | tf_op | source)
XLA Modules:
  0.0 360.1 jit_solution(11399913175671601973)
XLA Ops:
  8.3 3.9 %collective-permute-start = (f32[16,1,1280]{2,0,1:T(8,128)S(1)}, f32[16,1,1280]{2,0,1:T(8,128)S(1)}, u32[]{:S(2)}, u32[]{:S(2)}) collective-permute-start(f32[16,1,1280]{2,0,1:T(8,128)S(1)} %get-tuple-element.79), channel_id=1, source_target_pairs={{0,1},{1,2},{2,3},{3,4},{4,5},{5,6},{6,7},{7,8},{8,9},{9,10},{10,1... | collective-permute-start | bytes 245768 | tf_op jit(solution)/shard_map/ppermute | solution.py:16
  22.1 3.7 %collective-permute-done.3 = f32[16,1,1280]{2,0,1:T(8,128)S(1)} collective-permute-done((f32[16,1,1280]{2,0,1:T(8,128)S(1)}, f32[16,1,1280]{2,0,1:T(8,128)S(1)}, u32[]{:S(2)}, u32[]{:S(2)}) %collective-permute-start.3) | collective-permute-done | bytes 81952 | tf_op jit(solution)/shard_map/ppermute | solution.py:19
  25.9 5.0 %collective-permute-start.4 = (f32[16,1,1280]{2,0,1:T(8,128)S(1)}, f32[16,1,1280]{2,0,1:T(8,128)S(1)}, u32[]{:S(2)}, u32[]{:S(2)}) collective-permute-start(f32[16,1,1280]{2,0,1:T(8,128)S(1)} %get-tuple-element.75), channel_id=1, source_target_pairs={{0,1},{1,2},{2,3},{3,4},{4,5},{5,6},{6,7},{7,8},{8,9},{9,10},{10,1... | collective-permute-start | bytes 245768 | tf_op jit(solution)/shard_map/ppermute | solution.py:16
  32.4 3.7 %collective-permute-done.5 = f32[16,1,1280]{2,0,1:T(8,128)S(1)} collective-permute-done((f32[16,1,1280]{2,0,1:T(8,128)S(1)}, f32[16,1,1280]{2,0,1:T(8,128)S(1)}, u32[]{:S(2)}, u32[]{:S(2)}) %collective-permute-start.5) | collective-permute-done | bytes 81952 | tf_op jit(solution)/shard_map/ppermute | solution.py:19
  36.2 4.0 %collective-permute-start.6 = (bf16[16,1,1280]{2,0,1:T(8,128)(2,1)S(1)}, bf16[16,1,1280]{2,0,1:T(8,128)(2,1)S(1)}, u32[]{:S(2)}, u32[]{:S(2)}) collective-permute-start(bf16[16,1,1280]{2,0,1:T(8,128)(2,1)S(1)} %get-tuple-element.83), channel_id=1, source_target_pairs={{0,1},{1,2},{2,3},{3,4},{4,5},{5,6},{6,7},{7,8},{8,9},{9,10},{10,1... | collective-permute-start | bytes 122888 | tf_op jit(solution)/shard_map/ppermute | solution.py:16
  45.2 4.0 %fusion.8 = f32[16,6,2560]{2,0,1:T(8,128)S(1)} fusion(bf16[1280,2560]{1,0:T(8,128)(2,1)} %param.17, bf16[16,1,1280]{2,0,1:T(8,128)(2,1)S(1)} %collective-permute-done.7, bf16[16,4,1280]{2,0,1:T(8,128)(2,1)S(1)} %fusion.56, bf16[16,1,1280]{2,0,1:T(8,128)(2,1)S(1)} %collective-permute-done.6), kind=kOutput, calls=%fused_computation.10 | convolution fusion | flops 629391360 | bytes 7782400 | tf_op jit(solution)/shard_map/dot_general | solution.py:79
  54.1 38.6 %reduce-scatter.7.cloned.1.call-done = f32[320,16]{1,0:T(8,128)} async-done(((f32[2560,16]{1,0:T(8,128)}), f32[320,16]{1,0:T(8,128)}) %reduce-scatter.7.cloned.1.call-update) | async-done | bytes 20496
  95.9 9.8 %all-to-all-start = ((f32[128,1,8]{2,1,0:T(1,128)}), f32[128,1,8]{2,1,0:T(1,128)S(1)}, u32[]{:S(2)}, u32[]{:S(2)}) async-start(f32[128,1,8]{2,1,0:T(1,128)} %copy.126), calls=%async_computation | async-start | bytes 131072 | tf_op jit(solution)/shard_map/all_to_all | solution.py:182
  106.5 8.9 %all-to-all-done = f32[128,1,8]{2,1,0:T(1,128)S(1)} async-done(((f32[128,1,8]{2,1,0:T(1,128)}), f32[128,1,8]{2,1,0:T(1,128)S(1)}, u32[]{:S(2)}, u32[]{:S(2)}) %all-to-all-start) | async-done | bytes 4128 | tf_op jit(solution)/shard_map/all_to_all | solution.py:182
  116.5 4.3 %all-to-all-start.1 = ((f32[128,8,8]{2,1,0:T(8,128)}), f32[128,8,8]{2,1,0:T(8,128)S(1)}, u32[]{:S(2)}, u32[]{:S(2)}) async-start(f32[128,8,8]{2,1,0:T(8,128)} %bitcast.22), calls=%async_computation.1 | async-start | bytes 1048576 | tf_op jit(solution)/shard_map/all_to_all | solution.py:187
  120.8 14.1 %all-to-all-done.1 = f32[128,8,8]{2,1,0:T(8,128)S(1)} async-done(((f32[128,8,8]{2,1,0:T(8,128)}), f32[128,8,8]{2,1,0:T(8,128)S(1)}, u32[]{:S(2)}, u32[]{:S(2)}) %all-to-all-start.1) | async-done | bytes 32800 | tf_op jit(solution)/shard_map/all_to_all | solution.py:187
  135.1 11.3 %fusion.19 = f32[16,8,320]{2,0,1:T(8,128)S(1)} fusion(f32[128,8,8]{0,2,1:T(8,128)S(1)} %bitcast.162, s32[128,8,8]{0,2,1:T(8,128)S(1)} %get-tuple-element.89, f32[128,8,8]{0,2,1:T(8,128)S(1)} %get-tuple-element.96, s32[128,8,8]{0,2,1:T(8,128)S(1)} %get-tuple-element.90, f32[128,8,8]{0,2,1:T(8,128)S(1)} %broadcast_select_fusion, ...), kind=kOutput, calls=%fused_computation.31 | convolution fusion | flops 517210112 | bytes 458752 | tf_op jit(solution)/shard_map/bmsr,bmsc->rmc/dot_general | solution.py:131
  153.3 3.9 %collective-permute-done.9 = f32[16,1,2560]{2,0,1:T(8,128)S(1)} collective-permute-done((f32[16,1,2560]{2,0,1:T(8,128)S(1)}, f32[16,1,2560]{2,0,1:T(8,128)S(1)}, u32[]{:S(2)}, u32[]{:S(2)}) %collective-permute-start.9) | collective-permute-done | bytes 163872 | tf_op jit(solution)/shard_map/ppermute | solution.py:19
  167.3 3.9 %collective-permute-start.12 = (f32[16,1,1280]{2,0,1:T(8,128)S(1)}, f32[16,1,1280]{2,0,1:T(8,128)S(1)}, u32[]{:S(2)}, u32[]{:S(2)}) collective-permute-start(f32[16,1,1280]{2,0,1:T(8,128)S(1)} %get-tuple-element.71), channel_id=1, source_target_pairs={{0,1},{1,2},{2,3},{3,4},{4,5},{5,6},{6,7},{7,8},{8,9},{9,10},{10,1... | collective-permute-start | bytes 245768 | tf_op jit(solution)/shard_map/ppermute | solution.py:16
  176.5 4.3 %collective-permute-start.14 = (f32[16,1,1280]{2,0,1:T(8,128)S(1)}, f32[16,1,1280]{2,0,1:T(8,128)S(1)}, u32[]{:S(2)}, u32[]{:S(2)}) collective-permute-start(f32[16,1,1280]{2,0,1:T(8,128)S(1)} %get-tuple-element.69), channel_id=1, source_target_pairs={{0,1},{1,2},{2,3},{3,4},{4,5},{5,6},{6,7},{7,8},{8,9},{9,10},{10,1... | collective-permute-start | bytes 245768 | tf_op jit(solution)/shard_map/ppermute | solution.py:16
  186.7 3.7 %collective-permute-start.16 = (f32[16,1,1280]{2,0,1:T(8,128)S(1)}, f32[16,1,1280]{2,0,1:T(8,128)S(1)}, u32[]{:S(2)}, u32[]{:S(2)}) collective-permute-start(f32[16,1,1280]{2,0,1:T(8,128)S(1)} %get-tuple-element.67), channel_id=1, source_target_pairs={{0,1},{1,2},{2,3},{3,4},{4,5},{5,6},{6,7},{7,8},{8,9},{9,10},{10,1... | collective-permute-start | bytes 245768 | tf_op jit(solution)/shard_map/ppermute | solution.py:16
  195.7 4.0 %collective-permute-start.18 = (f32[16,1,1280]{2,0,1:T(8,128)S(1)}, f32[16,1,1280]{2,0,1:T(8,128)S(1)}, u32[]{:S(2)}, u32[]{:S(2)}) collective-permute-start(f32[16,1,1280]{2,0,1:T(8,128)S(1)} %get-tuple-element.65), channel_id=1, source_target_pairs={{0,1},{1,2},{2,3},{3,4},{4,5},{5,6},{6,7},{7,8},{8,9},{9,10},{10,1... | collective-permute-start | bytes 245768 | tf_op jit(solution)/shard_map/ppermute | solution.py:16
  205.0 4.0 %collective-permute-start.20 = (f32[16,1,1280]{2,0,1:T(8,128)S(1)}, f32[16,1,1280]{2,0,1:T(8,128)S(1)}, u32[]{:S(2)}, u32[]{:S(2)}) collective-permute-start(f32[16,1,1280]{2,0,1:T(8,128)S(1)} %get-tuple-element.63), channel_id=1, source_target_pairs={{0,1},{1,2},{2,3},{3,4},{4,5},{5,6},{6,7},{7,8},{8,9},{9,10},{10,1... | collective-permute-start | bytes 245768 | tf_op jit(solution)/shard_map/ppermute | solution.py:16
  214.3 4.0 %collective-permute-start.22 = (bf16[16,1,1280]{2,0,1:T(8,128)(2,1)S(1)}, bf16[16,1,1280]{2,0,1:T(8,128)(2,1)S(1)}, u32[]{:S(2)}, u32[]{:S(2)}) collective-permute-start(bf16[16,1,1280]{2,0,1:T(8,128)(2,1)S(1)} %get-tuple-element.81), channel_id=1, source_target_pairs={{0,1},{1,2},{2,3},{3,4},{4,5},{5,6},{6,7},{7,8},{8,9},{9,10},{10,1... | collective-permute-start | bytes 122888 | tf_op jit(solution)/shard_map/ppermute | solution.py:16
  220.6 18.2 %all-to-all-start.2 = ((f32[128,8,8]{2,1,0:T(8,128)}), f32[128,8,8]{2,1,0:T(8,128)S(1)}, u32[]{:S(2)}, u32[]{:S(2)}) async-start(f32[128,8,8]{2,1,0:T(8,128)} %bitcast.31), calls=%async_computation.2 | async-start | bytes 1048576 | tf_op jit(solution)/shard_map/all_to_all | solution.py:190
  238.9 4.0 %fusion.4 = f32[16,6,2560]{2,0,1:T(8,128)S(1)} fusion(bf16[1280,2560]{1,0:T(8,128)(2,1)} %param.17, bf16[16,1,1280]{2,0,1:T(8,128)(2,1)S(1)} %collective-permute-done.23, bf16[16,4,1280]{2,0,1:T(8,128)(2,1)S(1)} %fusion.30, bf16[16,1,1280]{2,0,1:T(8,128)(2,1)S(1)} %collective-permute-done.22), kind=kOutput, calls=%fused_computation.6 | convolution fusion | flops 629391360 | bytes 7782400 | tf_op jit(solution)/shard_map/dot_general | solution.py:79
  246.6 6.3 %all-to-all-done.2 = f32[128,8,8]{2,1,0:T(8,128)S(1)} async-done(((f32[128,8,8]{2,1,0:T(8,128)}), f32[128,8,8]{2,1,0:T(8,128)S(1)}, u32[]{:S(2)}, u32[]{:S(2)}) %all-to-all-start.2) | async-done | bytes 32800 | tf_op jit(solution)/shard_map/all_to_all | solution.py:190
  253.0 25.0 %reduce-scatter.9.cloned.1.call-done = f32[320,16]{1,0:T(8,128)} async-done(((f32[2560,16]{1,0:T(8,128)}), f32[320,16]{1,0:T(8,128)}) %reduce-scatter.9.cloned.1.call-update) | async-done | bytes 20496
  282.0 67.6 %all-reduce.3 = (f32[]{:T(128)}, f32[]{:T(128)}) all-reduce(f32[]{:T(128)} %get-tuple-element.40, f32[]{:T(128)} %fusion.103), channel_id=1, replica_groups=mesh['member'=8,'tile'=16] {'member','tile'}, use_global_device_ids=true, to_apply=%region_4.5 | all-reduce | flops 2 | bytes 16 | tf_op jit(solution)/shard_map/psum | solution.py:144
  (131 shorter events, 82.0 us)
Async XLA Ops:
  7.2 85.5 %reduce-scatter.7.cloned.1.call-start = ((), (), s32[]{:S(2)}) async-start(), calls=%async_computation.5 | async-start | bytes 1474560
  8.3 5.4 %collective-permute-start = (f32[16,1,1280]{2,0,1:T(8,128)S(1)}, f32[16,1,1280]{2,0,1:T(8,128)S(1)}, u32[]{:S(2)}, u32[]{:S(2)}) collective-permute-start(f32[16,1,1280]{2,0,1:T(8,128)S(1)} %get-tuple-element.79), channel_id=1, source_target_pairs={{0,1},{1,2},{2,3},{3,4},{4,5},{5,6},{6,7},{7,8},{8,9},{9,10},{10,1... | collective-permute-start | bytes 245768 | tf_op jit(solution)/shard_map/ppermute | solution.py:16
  12.2 5.2 %collective-permute-start.1 = (f32[16,1,1280]{2,0,1:T(8,128)S(1)}, f32[16,1,1280]{2,0,1:T(8,128)S(1)}, u32[]{:S(2)}, u32[]{:S(2)}) collective-permute-start(f32[16,1,1280]{2,0,1:T(8,128)S(1)} %get-tuple-element.80), channel_id=1, source_target_pairs={{1,0},{2,1},{3,2},{4,3},{5,4},{6,5},{7,6},{8,7},{9,8},{10,9},{11,1... | collective-permute-start | bytes 245768 | tf_op jit(solution)/shard_map/ppermute | solution.py:19
  20.6 5.2 %collective-permute-start.3 = (f32[16,1,1280]{2,0,1:T(8,128)S(1)}, f32[16,1,1280]{2,0,1:T(8,128)S(1)}, u32[]{:S(2)}, u32[]{:S(2)}) collective-permute-start(f32[16,1,1280]{2,0,1:T(8,128)S(1)} %get-tuple-element.78), channel_id=1, source_target_pairs={{1,0},{2,1},{3,2},{4,3},{5,4},{6,5},{7,6},{8,7},{9,8},{10,9},{11,1... | collective-permute-start | bytes 245768 | tf_op jit(solution)/shard_map/ppermute | solution.py:19
  25.9 6.5 %collective-permute-start.4 = (f32[16,1,1280]{2,0,1:T(8,128)S(1)}, f32[16,1,1280]{2,0,1:T(8,128)S(1)}, u32[]{:S(2)}, u32[]{:S(2)}) collective-permute-start(f32[16,1,1280]{2,0,1:T(8,128)S(1)} %get-tuple-element.75), channel_id=1, source_target_pairs={{0,1},{1,2},{2,3},{3,4},{4,5},{5,6},{6,7},{7,8},{8,9},{9,10},{10,1... | collective-permute-start | bytes 245768 | tf_op jit(solution)/shard_map/ppermute | solution.py:16
  30.9 5.2 %collective-permute-start.5 = (f32[16,1,1280]{2,0,1:T(8,128)S(1)}, f32[16,1,1280]{2,0,1:T(8,128)S(1)}, u32[]{:S(2)}, u32[]{:S(2)}) collective-permute-start(f32[16,1,1280]{2,0,1:T(8,128)S(1)} %get-tuple-element.76), channel_id=1, source_target_pairs={{1,0},{2,1},{3,2},{4,3},{5,4},{6,5},{7,6},{8,7},{9,8},{10,9},{11,1... | collective-permute-start | bytes 245768 | tf_op jit(solution)/shard_map/ppermute | solution.py:19
  36.2 5.4 %collective-permute-start.6 = (bf16[16,1,1280]{2,0,1:T(8,128)(2,1)S(1)}, bf16[16,1,1280]{2,0,1:T(8,128)(2,1)S(1)}, u32[]{:S(2)}, u32[]{:S(2)}) collective-permute-start(bf16[16,1,1280]{2,0,1:T(8,128)(2,1)S(1)} %get-tuple-element.83), channel_id=1, source_target_pairs={{0,1},{1,2},{2,3},{3,4},{4,5},{5,6},{6,7},{7,8},{8,9},{9,10},{10,1... | collective-permute-start | bytes 122888 | tf_op jit(solution)/shard_map/ppermute | solution.py:16
  95.9 19.6 %all-to-all-start = ((f32[128,1,8]{2,1,0:T(1,128)}), f32[128,1,8]{2,1,0:T(1,128)S(1)}, u32[]{:S(2)}, u32[]{:S(2)}) async-start(f32[128,1,8]{2,1,0:T(1,128)} %copy.126), calls=%async_computation | async-start | bytes 131072 | tf_op jit(solution)/shard_map/all_to_all | solution.py:182
  116.5 18.4 %all-to-all-start.1 = ((f32[128,8,8]{2,1,0:T(8,128)}), f32[128,8,8]{2,1,0:T(8,128)S(1)}, u32[]{:S(2)}, u32[]{:S(2)}) async-start(f32[128,8,8]{2,1,0:T(8,128)} %bitcast.22), calls=%async_computation.1 | async-start | bytes 1048576 | tf_op jit(solution)/shard_map/all_to_all | solution.py:187
  147.9 5.4 %collective-permute-start.8 = (f32[16,1,2560]{2,0,1:T(8,128)S(1)}, f32[16,1,2560]{2,0,1:T(8,128)S(1)}, u32[]{:S(2)}, u32[]{:S(2)}) collective-permute-start(f32[16,1,2560]{2,0,1:T(8,128)S(1)} %get-tuple-element.54), channel_id=1, source_target_pairs={{0,1},{1,2},{2,3},{3,4},{4,5},{5,6},{6,7},{7,8},{8,9},{9,10},{10,1... | collective-permute-start | bytes 491528 | tf_op jit(solution)/shard_map/ppermute | solution.py:16
  150.4 6.8 %collective-permute-start.9 = (f32[16,1,2560]{2,0,1:T(8,128)S(1)}, f32[16,1,2560]{2,0,1:T(8,128)S(1)}, u32[]{:S(2)}, u32[]{:S(2)}) collective-permute-start(f32[16,1,2560]{2,0,1:T(8,128)S(1)} %get-tuple-element.53), channel_id=1, source_target_pairs={{1,0},{2,1},{3,2},{4,3},{5,4},{6,5},{7,6},{8,7},{9,8},{10,9},{11,1... | collective-permute-start | bytes 491528 | tf_op jit(solution)/shard_map/ppermute | solution.py:19
  162.0 5.2 %collective-permute-start.11 = (f32[16,1,1280]{2,0,1:T(8,128)S(1)}, f32[16,1,1280]{2,0,1:T(8,128)S(1)}, u32[]{:S(2)}, u32[]{:S(2)}) collective-permute-start(f32[16,1,1280]{2,0,1:T(8,128)S(1)} %get-tuple-element.74), channel_id=1, source_target_pairs={{1,0},{2,1},{3,2},{4,3},{5,4},{6,5},{7,6},{8,7},{9,8},{10,9},{11,1... | collective-permute-start | bytes 245768 | tf_op jit(solution)/shard_map/ppermute | solution.py:19
  167.3 5.4 %collective-permute-start.12 = (f32[16,1,1280]{2,0,1:T(8,128)S(1)}, f32[16,1,1280]{2,0,1:T(8,128)S(1)}, u32[]{:S(2)}, u32[]{:S(2)}) collective-permute-start(f32[16,1,1280]{2,0,1:T(8,128)S(1)} %get-tuple-element.71), channel_id=1, source_target_pairs={{0,1},{1,2},{2,3},{3,4},{4,5},{5,6},{6,7},{7,8},{8,9},{9,10},{10,1... | collective-permute-start | bytes 245768 | tf_op jit(solution)/shard_map/ppermute | solution.py:16
  171.2 5.2 %collective-permute-start.13 = (f32[16,1,1280]{2,0,1:T(8,128)S(1)}, f32[16,1,1280]{2,0,1:T(8,128)S(1)}, u32[]{:S(2)}, u32[]{:S(2)}) collective-permute-start(f32[16,1,1280]{2,0,1:T(8,128)S(1)} %get-tuple-element.72), channel_id=1, source_target_pairs={{1,0},{2,1},{3,2},{4,3},{5,4},{6,5},{7,6},{8,7},{9,8},{10,9},{11,1... | collective-permute-start | bytes 245768 | tf_op jit(solution)/shard_map/ppermute | solution.py:19
  176.5 5.8 %collective-permute-start.14 = (f32[16,1,1280]{2,0,1:T(8,128)S(1)}, f32[16,1,1280]{2,0,1:T(8,128)S(1)}, u32[]{:S(2)}, u32[]{:S(2)}) collective-permute-start(f32[16,1,1280]{2,0,1:T(8,128)S(1)} %get-tuple-element.69), channel_id=1, source_target_pairs={{0,1},{1,2},{2,3},{3,4},{4,5},{5,6},{6,7},{7,8},{8,9},{9,10},{10,1... | collective-permute-start | bytes 245768 | tf_op jit(solution)/shard_map/ppermute | solution.py:16
  180.8 5.2 %collective-permute-start.15 = (f32[16,1,1280]{2,0,1:T(8,128)S(1)}, f32[16,1,1280]{2,0,1:T(8,128)S(1)}, u32[]{:S(2)}, u32[]{:S(2)}) collective-permute-start(f32[16,1,1280]{2,0,1:T(8,128)S(1)} %get-tuple-element.70), channel_id=1, source_target_pairs={{1,0},{2,1},{3,2},{4,3},{5,4},{6,5},{7,6},{8,7},{9,8},{10,9},{11,1... | collective-permute-start | bytes 245768 | tf_op jit(solution)/shard_map/ppermute | solution.py:19
  186.7 5.2 %collective-permute-start.16 = (f32[16,1,1280]{2,0,1:T(8,128)S(1)}, f32[16,1,1280]{2,0,1:T(8,128)S(1)}, u32[]{:S(2)}, u32[]{:S(2)}) collective-permute-start(f32[16,1,1280]{2,0,1:T(8,128)S(1)} %get-tuple-element.67), channel_id=1, source_target_pairs={{0,1},{1,2},{2,3},{3,4},{4,5},{5,6},{6,7},{7,8},{8,9},{9,10},{10,1... | collective-permute-start | bytes 245768 | tf_op jit(solution)/shard_map/ppermute | solution.py:16
  190.5 5.2 %collective-permute-start.17 = (f32[16,1,1280]{2,0,1:T(8,128)S(1)}, f32[16,1,1280]{2,0,1:T(8,128)S(1)}, u32[]{:S(2)}, u32[]{:S(2)}) collective-permute-start(f32[16,1,1280]{2,0,1:T(8,128)S(1)} %get-tuple-element.68), channel_id=1, source_target_pairs={{1,0},{2,1},{3,2},{4,3},{5,4},{6,5},{7,6},{8,7},{9,8},{10,9},{11,1... | collective-permute-start | bytes 245768 | tf_op jit(solution)/shard_map/ppermute | solution.py:19
  195.7 5.5 %collective-permute-start.18 = (f32[16,1,1280]{2,0,1:T(8,128)S(1)}, f32[16,1,1280]{2,0,1:T(8,128)S(1)}, u32[]{:S(2)}, u32[]{:S(2)}) collective-permute-start(f32[16,1,1280]{2,0,1:T(8,128)S(1)} %get-tuple-element.65), channel_id=1, source_target_pairs={{0,1},{1,2},{2,3},{3,4},{4,5},{5,6},{6,7},{7,8},{8,9},{9,10},{10,1... | collective-permute-start | bytes 245768 | tf_op jit(solution)/shard_map/ppermute | solution.py:16
  205.0 5.5 %collective-permute-start.20 = (f32[16,1,1280]{2,0,1:T(8,128)S(1)}, f32[16,1,1280]{2,0,1:T(8,128)S(1)}, u32[]{:S(2)}, u32[]{:S(2)}) collective-permute-start(f32[16,1,1280]{2,0,1:T(8,128)S(1)} %get-tuple-element.63), channel_id=1, source_target_pairs={{0,1},{1,2},{2,3},{3,4},{4,5},{5,6},{6,7},{7,8},{8,9},{9,10},{10,1... | collective-permute-start | bytes 245768 | tf_op jit(solution)/shard_map/ppermute | solution.py:16
  214.3 24.6 %collective-permute-start.22 = (bf16[16,1,1280]{2,0,1:T(8,128)(2,1)S(1)}, bf16[16,1,1280]{2,0,1:T(8,128)(2,1)S(1)}, u32[]{:S(2)}, u32[]{:S(2)}) collective-permute-start(bf16[16,1,1280]{2,0,1:T(8,128)(2,1)S(1)} %get-tuple-element.81), channel_id=1, source_target_pairs={{0,1},{1,2},{2,3},{3,4},{4,5},{5,6},{6,7},{7,8},{8,9},{9,10},{10,1... | collective-permute-start | bytes 122888 | tf_op jit(solution)/shard_map/ppermute | solution.py:16
  218.4 20.5 %collective-permute-start.23 = (bf16[16,1,1280]{2,0,1:T(8,128)(2,1)S(1)}, bf16[16,1,1280]{2,0,1:T(8,128)(2,1)S(1)}, u32[]{:S(2)}, u32[]{:S(2)}) collective-permute-start(bf16[16,1,1280]{2,0,1:T(8,128)(2,1)S(1)} %get-tuple-element.82), channel_id=1, source_target_pairs={{1,0},{2,1},{3,2},{4,3},{5,4},{6,5},{7,6},{8,7},{9,8},{10,9},{11,1... | collective-permute-start | bytes 122888 | tf_op jit(solution)/shard_map/ppermute | solution.py:19
  220.6 32.3 %all-to-all-start.2 = ((f32[128,8,8]{2,1,0:T(8,128)}), f32[128,8,8]{2,1,0:T(8,128)S(1)}, u32[]{:S(2)}, u32[]{:S(2)}) async-start(f32[128,8,8]{2,1,0:T(8,128)} %bitcast.31), calls=%async_computation.2 | async-start | bytes 1048576 | tf_op jit(solution)/shard_map/all_to_all | solution.py:190
  238.8 39.2 %reduce-scatter.9.cloned.1.call-start = ((), (), s32[]{:S(2)}) async-start(), calls=%async_computation.6 | async-start | bytes 1474560
  (16 other events, 300.3 us)
Sparse Core Ops, SparseCore 0:
  54.1 38.4 reduce-scatter.6
  246.7 31.3 reduce-scatter.8
where the time goes:
time: 361 us; the launch traced here: 360 us
  waiting for transfers between devices  137 us (38%)
  starting transfers between devices  93.4 us (26%)
  blocking collectives  67.6 us (19%)
  matrix products  25.3 us (7%)
  between operations  17.3 us (5%)
  local copies, waits for them, and re-layouts  12 us (3%)
  other arithmetic  7.7 us (2%)
    psum x1, blocking collectives, global_sum(): return lax.psum(values, ('member', 'tile'))  67.6 us
    unnamed x4, waiting for transfers between devices  63.6 us
    ppermute x12, starting transfers between devices, padded_2(): lax.ppermute(lax.slice_in_dim(block, block.shape[dim] - width, None, axis...  45.2 us
    ppermute x12, waiting for transfers between devices, padded_2(): lax.ppermute(lax.slice_in_dim(block, 0, width, axis=dim), axis, backward)  41.1 us
    all_to_all x1, starting transfers between devices, shards(): lax.all_to_all(fan_out(obs_weight), ('member', 'tile'), split_axis=0, con...  18.2 us
    ppermute x12, starting transfers between devices, padded_2(): lax.ppermute(lax.slice_in_dim(block, 0, width, axis=dim), axis, backward)  15.7 us
    all_to_all x1, waiting for transfers between devices, shards(): lax.all_to_all(fan_out(residual), ('member', 'tile'), split_axis=0, conca...  14.1 us
    dot_general x1, matrix products, spread_tile(): jnp.einsum('bmsr,bmsc->rmc', weighted, column_factor, precision=lax.Preci...  11.3 us
  transfers between devices with their start and end apart: 29, of which 26 were waited for; matrix products, arithmetic and copies ran while one was open for 3% of the time, Pallas kernels for 0%

commit v1 on v0

--- a/solution.py
+++ b/solution.py
@@ -141,7 +141,7 @@
 
 
 def global_sum(values):
-    return lax.psum(values, ("member", "tile"))
+    return lax.psum(lax.psum(values, "member"), "tile")
 
 
 def shards(

time: 361 us -> 350 us (0.970)
  the two profiles are of different devices: /device:TPU:1 before, /device:TPU:0 now
where the time goes in v1:
time: 350 us; the launch traced here: 349 us
  waiting for transfers between devices  149 us (43%)
  starting transfers between devices  83.7 us (24%)
  blocking collectives  54.6 us (16%)
  matrix products  25.3 us (7%)
  between operations  17.3 us (5%)
  local copies, waits for them, and re-layouts  12 us (3%)
  other arithmetic  7.7 us (2%)
    unnamed x4, waiting for transfers between devices  64.4 us
    psum x2, blocking collectives, global_sum(): return lax.psum(lax.psum(values, 'member'), 'tile')  54.6 us
    ppermute x12, waiting for transfers between devices, padded_2(): lax.ppermute(lax.slice_in_dim(block, 0, width, axis=dim), axis, backward)  47.2 us
    ppermute x12, starting transfers between devices, padded_2(): lax.ppermute(lax.slice_in_dim(block, block.shape[dim] - width, None, axis...  46.7 us
    ppermute x12, starting transfers between devices, padded_2(): lax.ppermute(lax.slice_in_dim(block, 0, width, axis=dim), axis, backward)  15.7 us
    all_to_all x1, waiting for transfers between devices, shards(): lax.all_to_all(fan_out(residual), ('member', 'tile'), split_axis=0, conca...  13.4 us
    dot_general x1, matrix products, spread_tile(): jnp.einsum('bmsr,bmsc->rmc', weighted, column_factor, precision=lax.Preci...  11.3 us
    ppermute x12, waiting for transfers between devices, padded_2(): lax.ppermute(lax.slice_in_dim(block, block.shape[dim] - width, None, axis...  9.15 us
  transfers between devices with their start and end apart: 29, of which 27 were waited for; matrix products, arithmetic and copies ran while one was open for 3% of the time, Pallas kernels for 0%

profile of v1, /device:TPU:0, one launch (start us, length us, event | category | flops | bytes accessed | tf_op | source)
XLA Modules:
  0.0 349.2 jit_solution(3955521573306211919)
XLA Ops:
  13.8 4.3 %collective-permute-done.1 = f32[16,1,1280]{2,0,1:T(8,128)S(1)} collective-permute-done((f32[16,1,1280]{2,0,1:T(8,128)S(1)}, f32[16,1,1280]{2,0,1:T(8,128)S(1)}, u32[]{:S(2)}, u32[]{:S(2)}) %collective-permute-start.1) | collective-permute-done | bytes 81952 | tf_op jit(solution)/shard_map/ppermute | solution.py:19
  23.7 4.3 %collective-permute-done.3 = f32[16,1,1280]{2,0,1:T(8,128)S(1)} collective-permute-done((f32[16,1,1280]{2,0,1:T(8,128)S(1)}, f32[16,1,1280]{2,0,1:T(8,128)S(1)}, u32[]{:S(2)}, u32[]{:S(2)}) %collective-permute-start.3) | collective-permute-done | bytes 81952 | tf_op jit(solution)/shard_map/ppermute | solution.py:19
  28.0 5.0 %collective-permute-start.4 = (f32[16,1,1280]{2,0,1:T(8,128)S(1)}, f32[16,1,1280]{2,0,1:T(8,128)S(1)}, u32[]{:S(2)}, u32[]{:S(2)}) collective-permute-start(f32[16,1,1280]{2,0,1:T(8,128)S(1)} %get-tuple-element.77), channel_id=1, source_target_pairs={{0,1},{1,2},{2,3},{3,4},{4,5},{5,6},{6,7},{7,8},{8,9},{9,10},{10,1... | collective-permute-start | bytes 245768 | tf_op jit(solution)/shard_map/ppermute | solution.py:16
  35.1 4.3 %collective-permute-done.5 = f32[16,1,1280]{2,0,1:T(8,128)S(1)} collective-permute-done((f32[16,1,1280]{2,0,1:T(8,128)S(1)}, f32[16,1,1280]{2,0,1:T(8,128)S(1)}, u32[]{:S(2)}, u32[]{:S(2)}) %collective-permute-start.5) | collective-permute-done | bytes 81952 | tf_op jit(solution)/shard_map/ppermute | solution.py:19
  45.2 4.2 %collective-permute-done.7 = bf16[16,1,1280]{2,0,1:T(8,128)(2,1)S(1)} collective-permute-done((bf16[16,1,1280]{2,0,1:T(8,128)(2,1)S(1)}, bf16[16,1,1280]{2,0,1:T(8,128)(2,1)S(1)}, u32[]{:S(2)}, u32[]{:S(2)}) %collective-permute-start.7) | collective-permute-done | bytes 40992 | tf_op jit(solution)/shard_map/ppermute | solution.py:19
  58.3 36.4 %reduce-scatter.7.cloned.1.call-done = f32[320,16]{1,0:T(8,128)} async-done(((f32[2560,16]{1,0:T(8,128)}), f32[320,16]{1,0:T(8,128)}) %reduce-scatter.7.cloned.1.call-update) | async-done | bytes 20496
  97.9 7.5 %all-to-all-start = ((f32[128,1,8]{2,1,0:T(1,128)}), f32[128,1,8]{2,1,0:T(1,128)S(1)}, u32[]{:S(2)}, u32[]{:S(2)}) async-start(f32[128,1,8]{2,1,0:T(1,128)} %copy.126), calls=%async_computation | async-start | bytes 131072 | tf_op jit(solution)/shard_map/all_to_all | solution.py:182
  106.2 8.6 %all-to-all-done = f32[128,1,8]{2,1,0:T(1,128)S(1)} async-done(((f32[128,1,8]{2,1,0:T(1,128)}), f32[128,1,8]{2,1,0:T(1,128)S(1)}, u32[]{:S(2)}, u32[]{:S(2)}) %all-to-all-start) | async-done | bytes 4128 | tf_op jit(solution)/shard_map/all_to_all | solution.py:182
  115.9 4.8 %all-to-all-start.1 = ((f32[128,8,8]{2,1,0:T(8,128)}), f32[128,8,8]{2,1,0:T(8,128)S(1)}, u32[]{:S(2)}, u32[]{:S(2)}) async-start(f32[128,8,8]{2,1,0:T(8,128)} %bitcast.22), calls=%async_computation.1 | async-start | bytes 1048576 | tf_op jit(solution)/shard_map/all_to_all | solution.py:187
  120.7 13.4 %all-to-all-done.1 = f32[128,8,8]{2,1,0:T(8,128)S(1)} async-done(((f32[128,8,8]{2,1,0:T(8,128)}), f32[128,8,8]{2,1,0:T(8,128)S(1)}, u32[]{:S(2)}, u32[]{:S(2)}) %all-to-all-start.1) | async-done | bytes 32800 | tf_op jit(solution)/shard_map/all_to_all | solution.py:187
  134.3 11.3 %fusion.19 = f32[16,8,320]{2,0,1:T(8,128)S(1)} fusion(f32[128,8,8]{0,2,1:T(8,128)S(1)} %bitcast.162, s32[128,8,8]{0,2,1:T(8,128)S(1)} %get-tuple-element.91, f32[128,8,8]{0,2,1:T(8,128)S(1)} %get-tuple-element.98, s32[128,8,8]{0,2,1:T(8,128)S(1)} %get-tuple-element.92, f32[128,8,8]{0,2,1:T(8,128)S(1)} %broadcast_select_fusion, ...), kind=kOutput, calls=%fused_computation.31 | convolution fusion | flops 517210112 | bytes 458752 | tf_op jit(solution)/shard_map/bmsr,bmsc->rmc/dot_general | solution.py:131
  153.3 4.2 %collective-permute-done.9 = f32[16,1,2560]{2,0,1:T(8,128)S(1)} collective-permute-done((f32[16,1,2560]{2,0,1:T(8,128)S(1)}, f32[16,1,2560]{2,0,1:T(8,128)S(1)}, u32[]{:S(2)}, u32[]{:S(2)}) %collective-permute-start.9) | collective-permute-done | bytes 163872 | tf_op jit(solution)/shard_map/ppermute | solution.py:19
  164.2 4.3 %collective-permute-done.11 = f32[16,1,1280]{2,0,1:T(8,128)S(1)} collective-permute-done((f32[16,1,1280]{2,0,1:T(8,128)S(1)}, f32[16,1,1280]{2,0,1:T(8,128)S(1)}, u32[]{:S(2)}, u32[]{:S(2)}) %collective-permute-start.11) | collective-permute-done | bytes 81952 | tf_op jit(solution)/shard_map/ppermute | solution.py:19
  168.6 5.4 %collective-permute-start.12 = (f32[16,1,1280]{2,0,1:T(8,128)S(1)}, f32[16,1,1280]{2,0,1:T(8,128)S(1)}, u32[]{:S(2)}, u32[]{:S(2)}) collective-permute-start(f32[16,1,1280]{2,0,1:T(8,128)S(1)} %get-tuple-element.73), channel_id=1, source_target_pairs={{0,1},{1,2},{2,3},{3,4},{4,5},{5,6},{6,7},{7,8},{8,9},{9,10},{10,1... | collective-permute-start | bytes 245768 | tf_op jit(solution)/shard_map/ppermute | solution.py:16
  176.0 4.3 %collective-permute-done.13 = f32[16,1,1280]{2,0,1:T(8,128)S(1)} collective-permute-done((f32[16,1,1280]{2,0,1:T(8,128)S(1)}, f32[16,1,1280]{2,0,1:T(8,128)S(1)}, u32[]{:S(2)}, u32[]{:S(2)}) %collective-permute-start.13) | collective-permute-done | bytes 81952 | tf_op jit(solution)/shard_map/ppermute | solution.py:19
  186.5 4.3 %collective-permute-done.15 = f32[16,1,1280]{2,0,1:T(8,128)S(1)} collective-permute-done((f32[16,1,1280]{2,0,1:T(8,128)S(1)}, f32[16,1,1280]{2,0,1:T(8,128)S(1)}, u32[]{:S(2)}, u32[]{:S(2)}) %collective-permute-start.15) | collective-permute-done | bytes 81952 | tf_op jit(solution)/shard_map/ppermute | solution.py:19
  197.6 4.3 %collective-permute-done.17 = f32[16,1,1280]{2,0,1:T(8,128)S(1)} collective-permute-done((f32[16,1,1280]{2,0,1:T(8,128)S(1)}, f32[16,1,1280]{2,0,1:T(8,128)S(1)}, u32[]{:S(2)}, u32[]{:S(2)}) %collective-permute-start.17) | collective-permute-done | bytes 81952 | tf_op jit(solution)/shard_map/ppermute | solution.py:19
  208.0 4.3 %collective-permute-done.19 = f32[16,1,1280]{2,0,1:T(8,128)S(1)} collective-permute-done((f32[16,1,1280]{2,0,1:T(8,128)S(1)}, f32[16,1,1280]{2,0,1:T(8,128)S(1)}, u32[]{:S(2)}, u32[]{:S(2)}) %collective-permute-start.19) | collective-permute-done | bytes 81952 | tf_op jit(solution)/shard_map/ppermute | solution.py:19
  218.8 4.4 %collective-permute-done.21 = f32[16,1,1280]{2,0,1:T(8,128)S(1)} collective-permute-done((f32[16,1,1280]{2,0,1:T(8,128)S(1)}, f32[16,1,1280]{2,0,1:T(8,128)S(1)}, u32[]{:S(2)}, u32[]{:S(2)}) %collective-permute-start.21) | collective-permute-done | bytes 81952 | tf_op jit(solution)/shard_map/ppermute | solution.py:19
  229.6 8.9 %all-to-all-start.2 = ((f32[128,8,8]{2,1,0:T(8,128)}), f32[128,8,8]{2,1,0:T(8,128)S(1)}, u32[]{:S(2)}, u32[]{:S(2)}) async-start(f32[128,8,8]{2,1,0:T(8,128)} %bitcast.31), calls=%async_computation.2 | async-start | bytes 1048576 | tf_op jit(solution)/shard_map/all_to_all | solution.py:190
  246.3 5.8 %all-to-all-done.2 = f32[128,8,8]{2,1,0:T(8,128)S(1)} async-done(((f32[128,8,8]{2,1,0:T(8,128)}), f32[128,8,8]{2,1,0:T(8,128)S(1)}, u32[]{:S(2)}, u32[]{:S(2)}) %all-to-all-start.2) | async-done | bytes 32800 | tf_op jit(solution)/shard_map/all_to_all | solution.py:190
  252.2 28.0 %reduce-scatter.9.cloned.1.call-done = f32[320,16]{1,0:T(8,128)} async-done(((f32[2560,16]{1,0:T(8,128)}), f32[320,16]{1,0:T(8,128)}) %reduce-scatter.9.cloned.1.call-update) | async-done | bytes 20496
  284.2 13.4 %all-reduce.4 = (f32[]{:T(128)}, f32[]{:T(128)}) all-reduce(f32[]{:T(128)} %get-tuple-element.42, f32[]{:T(128)} %fusion.103), channel_id=1, replica_groups=mesh['member'=8,'tile'=16] {'member'}, use_global_device_ids=true, to_apply=%region_4.5 | all-reduce | flops 2 | bytes 16 | tf_op jit(solution)/shard_map/psum | solution.py:144
  297.5 41.3 %all-reduce.3 = (f32[]{:T(128)}, f32[]{:T(128)}) all-reduce(f32[]{:T(128)} %get-tuple-element.40, f32[]{:T(128)} %get-tuple-element.41), channel_id=1, replica_groups=mesh['member'=8,'tile'=16] {'tile'}, use_global_device_ids=true, to_apply=%region_5.6 | all-reduce | flops 2 | bytes 16 | tf_op jit(solution)/shard_map/psum | solution.py:144
  (132 shorter events, 94.9 us)
Async XLA Ops:
  7.2 87.5 %reduce-scatter.7.cloned.1.call-start = ((), (), s32[]{:S(2)}) async-start(), calls=%async_computation.5 | async-start | bytes 1474560
  11.8 6.3 %collective-permute-start.1 = (f32[16,1,1280]{2,0,1:T(8,128)S(1)}, f32[16,1,1280]{2,0,1:T(8,128)S(1)}, u32[]{:S(2)}, u32[]{:S(2)}) collective-permute-start(f32[16,1,1280]{2,0,1:T(8,128)S(1)} %get-tuple-element.82), channel_id=1, source_target_pairs={{1,0},{2,1},{3,2},{4,3},{5,4},{6,5},{7,6},{8,7},{9,8},{10,9},{11,1... | collective-permute-start | bytes 245768 | tf_op jit(solution)/shard_map/ppermute | solution.py:19
  21.6 6.3 %collective-permute-start.3 = (f32[16,1,1280]{2,0,1:T(8,128)S(1)}, f32[16,1,1280]{2,0,1:T(8,128)S(1)}, u32[]{:S(2)}, u32[]{:S(2)}) collective-permute-start(f32[16,1,1280]{2,0,1:T(8,128)S(1)} %get-tuple-element.80), channel_id=1, source_target_pairs={{1,0},{2,1},{3,2},{4,3},{5,4},{6,5},{7,6},{8,7},{9,8},{10,9},{11,1... | collective-permute-start | bytes 245768 | tf_op jit(solution)/shard_map/ppermute | solution.py:19
  28.0 7.1 %collective-permute-start.4 = (f32[16,1,1280]{2,0,1:T(8,128)S(1)}, f32[16,1,1280]{2,0,1:T(8,128)S(1)}, u32[]{:S(2)}, u32[]{:S(2)}) collective-permute-start(f32[16,1,1280]{2,0,1:T(8,128)S(1)} %get-tuple-element.77), channel_id=1, source_target_pairs={{0,1},{1,2},{2,3},{3,4},{4,5},{5,6},{6,7},{7,8},{8,9},{9,10},{10,1... | collective-permute-start | bytes 245768 | tf_op jit(solution)/shard_map/ppermute | solution.py:16
  33.1 6.3 %collective-permute-start.5 = (f32[16,1,1280]{2,0,1:T(8,128)S(1)}, f32[16,1,1280]{2,0,1:T(8,128)S(1)}, u32[]{:S(2)}, u32[]{:S(2)}) collective-permute-start(f32[16,1,1280]{2,0,1:T(8,128)S(1)} %get-tuple-element.78), channel_id=1, source_target_pairs={{1,0},{2,1},{3,2},{4,3},{5,4},{6,5},{7,6},{8,7},{9,8},{10,9},{11,1... | collective-permute-start | bytes 245768 | tf_op jit(solution)/shard_map/ppermute | solution.py:19
  97.9 16.9 %all-to-all-start = ((f32[128,1,8]{2,1,0:T(1,128)}), f32[128,1,8]{2,1,0:T(1,128)S(1)}, u32[]{:S(2)}, u32[]{:S(2)}) async-start(f32[128,1,8]{2,1,0:T(1,128)} %copy.126), calls=%async_computation | async-start | bytes 131072 | tf_op jit(solution)/shard_map/all_to_all | solution.py:182
  115.9 18.2 %all-to-all-start.1 = ((f32[128,8,8]{2,1,0:T(8,128)}), f32[128,8,8]{2,1,0:T(8,128)S(1)}, u32[]{:S(2)}, u32[]{:S(2)}) async-start(f32[128,8,8]{2,1,0:T(8,128)} %bitcast.22), calls=%async_computation.1 | async-start | bytes 1048576 | tf_op jit(solution)/shard_map/all_to_all | solution.py:187
  147.0 6.2 %collective-permute-start.8 = (f32[16,1,2560]{2,0,1:T(8,128)S(1)}, f32[16,1,2560]{2,0,1:T(8,128)S(1)}, u32[]{:S(2)}, u32[]{:S(2)}) collective-permute-start(f32[16,1,2560]{2,0,1:T(8,128)S(1)} %get-tuple-element.56), channel_id=1, source_target_pairs={{0,1},{1,2},{2,3},{3,4},{4,5},{5,6},{6,7},{7,8},{8,9},{9,10},{10,1... | collective-permute-start | bytes 491528 | tf_op jit(solution)/shard_map/ppermute | solution.py:16
  149.8 7.7 %collective-permute-start.9 = (f32[16,1,2560]{2,0,1:T(8,128)S(1)}, f32[16,1,2560]{2,0,1:T(8,128)S(1)}, u32[]{:S(2)}, u32[]{:S(2)}) collective-permute-start(f32[16,1,2560]{2,0,1:T(8,128)S(1)} %get-tuple-element.55), channel_id=1, source_target_pairs={{1,0},{2,1},{3,2},{4,3},{5,4},{6,5},{7,6},{8,7},{9,8},{10,9},{11,1... | collective-permute-start | bytes 491528 | tf_op jit(solution)/shard_map/ppermute | solution.py:19
  162.2 6.3 %collective-permute-start.11 = (f32[16,1,1280]{2,0,1:T(8,128)S(1)}, f32[16,1,1280]{2,0,1:T(8,128)S(1)}, u32[]{:S(2)}, u32[]{:S(2)}) collective-permute-start(f32[16,1,1280]{2,0,1:T(8,128)S(1)} %get-tuple-element.76), channel_id=1, source_target_pairs={{1,0},{2,1},{3,2},{4,3},{5,4},{6,5},{7,6},{8,7},{9,8},{10,9},{11,1... | collective-permute-start | bytes 245768 | tf_op jit(solution)/shard_map/ppermute | solution.py:19
  168.6 7.4 %collective-permute-start.12 = (f32[16,1,1280]{2,0,1:T(8,128)S(1)}, f32[16,1,1280]{2,0,1:T(8,128)S(1)}, u32[]{:S(2)}, u32[]{:S(2)}) collective-permute-start(f32[16,1,1280]{2,0,1:T(8,128)S(1)} %get-tuple-element.73), channel_id=1, source_target_pairs={{0,1},{1,2},{2,3},{3,4},{4,5},{5,6},{6,7},{7,8},{8,9},{9,10},{10,1... | collective-permute-start | bytes 245768 | tf_op jit(solution)/shard_map/ppermute | solution.py:16
  174.0 6.3 %collective-permute-start.13 = (f32[16,1,1280]{2,0,1:T(8,128)S(1)}, f32[16,1,1280]{2,0,1:T(8,128)S(1)}, u32[]{:S(2)}, u32[]{:S(2)}) collective-permute-start(f32[16,1,1280]{2,0,1:T(8,128)S(1)} %get-tuple-element.74), channel_id=1, source_target_pairs={{1,0},{2,1},{3,2},{4,3},{5,4},{6,5},{7,6},{8,7},{9,8},{10,9},{11,1... | collective-permute-start | bytes 245768 | tf_op jit(solution)/shard_map/ppermute | solution.py:19
  180.4 6.1 %collective-permute-start.14 = (f32[16,1,1280]{2,0,1:T(8,128)S(1)}, f32[16,1,1280]{2,0,1:T(8,128)S(1)}, u32[]{:S(2)}, u32[]{:S(2)}) collective-permute-start(f32[16,1,1280]{2,0,1:T(8,128)S(1)} %get-tuple-element.71), channel_id=1, source_target_pairs={{0,1},{1,2},{2,3},{3,4},{4,5},{5,6},{6,7},{7,8},{8,9},{9,10},{10,1... | collective-permute-start | bytes 245768 | tf_op jit(solution)/shard_map/ppermute | solution.py:16
  184.5 6.3 %collective-permute-start.15 = (f32[16,1,1280]{2,0,1:T(8,128)S(1)}, f32[16,1,1280]{2,0,1:T(8,128)S(1)}, u32[]{:S(2)}, u32[]{:S(2)}) collective-permute-start(f32[16,1,1280]{2,0,1:T(8,128)S(1)} %get-tuple-element.72), channel_id=1, source_target_pairs={{1,0},{2,1},{3,2},{4,3},{5,4},{6,5},{7,6},{8,7},{9,8},{10,9},{11,1... | collective-permute-start | bytes 245768 | tf_op jit(solution)/shard_map/ppermute | solution.py:19
  191.5 6.1 %collective-permute-start.16 = (f32[16,1,1280]{2,0,1:T(8,128)S(1)}, f32[16,1,1280]{2,0,1:T(8,128)S(1)}, u32[]{:S(2)}, u32[]{:S(2)}) collective-permute-start(f32[16,1,1280]{2,0,1:T(8,128)S(1)} %get-tuple-element.69), channel_id=1, source_target_pairs={{0,1},{1,2},{2,3},{3,4},{4,5},{5,6},{6,7},{7,8},{8,9},{9,10},{10,1... | collective-permute-start | bytes 245768 | tf_op jit(solution)/shard_map/ppermute | solution.py:16
  195.6 6.3 %collective-permute-start.17 = (f32[16,1,1280]{2,0,1:T(8,128)S(1)}, f32[16,1,1280]{2,0,1:T(8,128)S(1)}, u32[]{:S(2)}, u32[]{:S(2)}) collective-permute-start(f32[16,1,1280]{2,0,1:T(8,128)S(1)} %get-tuple-element.70), channel_id=1, source_target_pairs={{1,0},{2,1},{3,2},{4,3},{5,4},{6,5},{7,6},{8,7},{9,8},{10,9},{11,1... | collective-permute-start | bytes 245768 | tf_op jit(solution)/shard_map/ppermute | solution.py:19
  202.0 6.1 %collective-permute-start.18 = (f32[16,1,1280]{2,0,1:T(8,128)S(1)}, f32[16,1,1280]{2,0,1:T(8,128)S(1)}, u32[]{:S(2)}, u32[]{:S(2)}) collective-permute-start(f32[16,1,1280]{2,0,1:T(8,128)S(1)} %get-tuple-element.67), channel_id=1, source_target_pairs={{0,1},{1,2},{2,3},{3,4},{4,5},{5,6},{6,7},{7,8},{8,9},{9,10},{10,1... | collective-permute-start | bytes 245768 | tf_op jit(solution)/shard_map/ppermute | solution.py:16
  206.0 6.3 %collective-permute-start.19 = (f32[16,1,1280]{2,0,1:T(8,128)S(1)}, f32[16,1,1280]{2,0,1:T(8,128)S(1)}, u32[]{:S(2)}, u32[]{:S(2)}) collective-permute-start(f32[16,1,1280]{2,0,1:T(8,128)S(1)} %get-tuple-element.68), channel_id=1, source_target_pairs={{1,0},{2,1},{3,2},{4,3},{5,4},{6,5},{7,6},{8,7},{9,8},{10,9},{11,1... | collective-permute-start | bytes 245768 | tf_op jit(solution)/shard_map/ppermute | solution.py:19
  212.4 6.4 %collective-permute-start.20 = (f32[16,1,1280]{2,0,1:T(8,128)S(1)}, f32[16,1,1280]{2,0,1:T(8,128)S(1)}, u32[]{:S(2)}, u32[]{:S(2)}) collective-permute-start(f32[16,1,1280]{2,0,1:T(8,128)S(1)} %get-tuple-element.65), channel_id=1, source_target_pairs={{0,1},{1,2},{2,3},{3,4},{4,5},{5,6},{6,7},{7,8},{8,9},{9,10},{10,1... | collective-permute-start | bytes 245768 | tf_op jit(solution)/shard_map/ppermute | solution.py:16
  216.5 6.8 %collective-permute-start.21 = (f32[16,1,1280]{2,0,1:T(8,128)S(1)}, f32[16,1,1280]{2,0,1:T(8,128)S(1)}, u32[]{:S(2)}, u32[]{:S(2)}) collective-permute-start(f32[16,1,1280]{2,0,1:T(8,128)S(1)} %get-tuple-element.66), channel_id=1, source_target_pairs={{1,0},{2,1},{3,2},{4,3},{5,4},{6,5},{7,6},{8,7},{9,8},{10,9},{11,1... | collective-permute-start | bytes 245768 | tf_op jit(solution)/shard_map/ppermute | solution.py:19
  223.3 15.3 %collective-permute-start.22 = (bf16[16,1,1280]{2,0,1:T(8,128)(2,1)S(1)}, bf16[16,1,1280]{2,0,1:T(8,128)(2,1)S(1)}, u32[]{:S(2)}, u32[]{:S(2)}) collective-permute-start(bf16[16,1,1280]{2,0,1:T(8,128)(2,1)S(1)} %get-tuple-element.83), channel_id=1, source_target_pairs={{0,1},{1,2},{2,3},{3,4},{4,5},{5,6},{6,7},{7,8},{8,9},{9,10},{10,1... | collective-permute-start | bytes 122888 | tf_op jit(solution)/shard_map/ppermute | solution.py:16
  227.4 11.2 %collective-permute-start.23 = (bf16[16,1,1280]{2,0,1:T(8,128)(2,1)S(1)}, bf16[16,1,1280]{2,0,1:T(8,128)(2,1)S(1)}, u32[]{:S(2)}, u32[]{:S(2)}) collective-permute-start(bf16[16,1,1280]{2,0,1:T(8,128)(2,1)S(1)} %get-tuple-element.84), channel_id=1, source_target_pairs={{1,0},{2,1},{3,2},{4,3},{5,4},{6,5},{7,6},{8,7},{9,8},{10,9},{11,1... | collective-permute-start | bytes 122888 | tf_op jit(solution)/shard_map/ppermute | solution.py:19
  229.6 22.5 %all-to-all-start.2 = ((f32[128,8,8]{2,1,0:T(8,128)}), f32[128,8,8]{2,1,0:T(8,128)S(1)}, u32[]{:S(2)}, u32[]{:S(2)}) async-start(f32[128,8,8]{2,1,0:T(8,128)} %bitcast.31), calls=%async_computation.2 | async-start | bytes 1048576 | tf_op jit(solution)/shard_map/all_to_all | solution.py:190
  238.5 41.7 %reduce-scatter.9.cloned.1.call-start = ((), (), s32[]{:S(2)}) async-start(), calls=%async_computation.6 | async-start | bytes 1474560
  (16 other events, 299.4 us)
Sparse Core Ops, SparseCore 0:
  58.3 36.3 reduce-scatter.6
  246.4 33.7 reduce-scatter.8
